TPU v7x, 32 devices: a whole 2x2x4 slice. The times are simulated.
32 devices in a mesh: groups: 2 (over y), feat: 4 (over z), layer: 2 (over x), tok: 2 (over core).
Axes of the slice: x: 2, y: 2, z: 4, core: 2. Of those that a mesh axis runs over, the one named last changes fastest.
Arguments:
- residual_in: float32 [256, 2, 1792], P('groups', 'tok', 'feat'), parts along dimension 0, may hold values from -6 to 6
- attn_scale: float32 [2, 256], P('layer', 'groups'), parts along dimension 1, may hold values from 0.4 to 2.5
- mlp_scale: float32 [2, 256], P('layer', 'groups'), parts along dimension 1, may hold values from 0.4 to 2.5
- patterns: bfloat16 [2, 8, 4, 64, 64], P('layer', None, 'groups'), parts along dimension 2, may hold values from 0.0029907227 to 0.059814453
- lengths: int32 [4], P('groups'), parts along dimension 0, may hold values from 16 to 64
- value_proj: bfloat16 [2, 2, 1792, 1024], P('layer', 'tok', None, 'feat'), may hold values from -0.09375 to 0.09375
- out_proj: bfloat16 [2, 4, 256, 2, 2, 1792], P('layer', None, None, None, 'tok', 'feat'), may hold values from -0.125 to 0.125
- enc_weight: bfloat16 [2, 2, 1792, 512], P('layer', 'tok', None, 'feat'), may hold values from -0.09375 to 0.09375
- enc_bias: float32 [2, 512], P('layer', 'feat'), may hold values from -3 to 3
- dec_weight: bfloat16 [2, 2, 512, 2, 1792], P('layer', None, None, 'tok', 'feat'), may hold values from -0.25 to 0.25
- errors: float32 [2, 256, 2, 1792], P('layer', 'groups', 'tok', 'feat'), parts along dimension 1, may hold values from -4 to 4
- clamp_mode: int32 [2, 16384], P('layer', 'feat'), may hold values from 0 to 2
- clamp_index: int32 [2, 16384], P('layer', 'feat'), may hold values from 0 to 63
- clamp_values: float32 [64], replicated, may hold values from 0.25 to 3
- active_blocks: int32 [2, 4], P('layer', 'feat'), may hold values from 0 to 31
Outputs:
- residual_out: float32 [2, 256, 2, 1792], P('layer', 'groups', 'tok', 'feat'), parts along dimension 1
- features: bfloat16 [2, 256, 512], P('layer', 'groups', 'feat'), parts along dimension 1
There are 2 independent parts, one for each index of `groups`. A program takes and returns all parts, laid end to end along the dimension named above; an argument that names none is the same for every part. Nothing has to cross between parts.
Inputs may be any that keep to these rules, and one draw needn't show every extreme that they name: `clamp_mode`: 0 leaves a feature free, 1 sets it to its table value, 2 multiplies it by its table value. `lengths`: positions at or past a prompt's length are padding.
All inputs are finite; a program needn't handle non-finite values.
Results may differ from a plain program's by a relative error of at most 0.018.
Values may be sent and summed in bfloat16 or wider, within the bound.
A program may use at most 64 MiB of HBM per device.

v0:
```python
import jax
import jax.numpy as jnp
from jax import lax
from jax.sharding import PartitionSpec as P


def passed_along(value, axis, steps):
    count = lax.axis_size(axis)
    initial, last = (max(0, -steps), min(count, count - steps))
    return lax.ppermute(value, axis, [(source, source + steps) for source in range(initial, last)])


def columns(normed_rows):
    return lax.all_gather(normed_rows, "feat", axis=1, tiled=True)


def halves(partial_sum):
    return lax.psum(partial_sum, "tok")


def pick_block(lookup_table, chosen, block_len):
    shaped = lookup_table.reshape(-1, block_len)
    return lax.dynamic_slice_in_dim(shaped, chosen, 1, 0)[0]


def local(
    residual_in,
    attn_scale,
    mlp_scale,
    patterns,
    lengths,
    value_proj,
    out_proj,
    enc_weight,
    enc_bias,
    dec_weight,
    errors,
    clamp_mode,
    clamp_index,
    clamp_values,
    active_blocks,
):
    layer_count = lax.axis_size("layer")
    my_layer = lax.axis_index("layer")
    my_range = lax.axis_index("feat")
    seq_len = patterns.shape[3]
    prompt_count = patterns.shape[2]
    head_dim = out_proj.shape[2]
    per_group = out_proj.shape[3]
    kv_cols = value_proj.shape[3]
    width_cols = residual_in.shape[2]
    block_len = enc_bias.shape[1]
    total_rows = residual_in.shape[0]
    split_count = 1
    block_rows = seq_len // split_count
    micro_count = prompt_count * split_count
    section_count = layer_count + micro_count - 1
    source_rows = residual_in[:, 0, :]
    error_rows = errors[0, :, 0, :]
    value_weight = value_proj[0, 0]
    out_weight = out_proj[0].reshape(-1, width_cols)
    enc_rows = enc_weight[0, 0]
    enc_shift = enc_bias[0]
    dec_rows = dec_weight[0, :, :, 0, :]
    chosen = active_blocks[0, 0]
    modes = pick_block(clamp_mode[0], chosen, block_len)
    table_pick = pick_block(clamp_index[0], chosen, block_len)
    table_ids = jnp.arange(clamp_values.shape[0], dtype=jnp.int32)
    levels = jnp.sum(
        jnp.where(table_pick[:, None] == table_ids[None, :], clamp_values[None, :], 0.0), axis=1
    )
    group_id = my_range * kv_cols // head_dim
    group_pat = lax.dynamic_slice_in_dim(patterns[0], group_id * per_group, per_group, 0)
    positions = jnp.arange(seq_len, dtype=jnp.int32)
    scale_attn = attn_scale[0]
    scale_mlp = mlp_scale[0]

    def add_heads(piece):
        return jnp.dot(piece, out_weight, preferred_element_type=jnp.float32)

    def add_writes(piece):
        return jnp.einsum("rf,tfc->trc", piece, dec_rows, preferred_element_type=jnp.float32)

    def section(step_num, carry):
        recv_rows, links, value_cache, kept_rows, kept_feats = carry
        micro_raw = step_num - my_layer
        is_live = (micro_raw >= 0) & (micro_raw < micro_count)
        micro_num = jnp.clip(micro_raw, 0, micro_count - 1)
        prompt_num = micro_num // split_count
        block_num = micro_num % split_count
        first_row = micro_num * block_rows
        first_pos = block_num * block_rows
        start_rows = lax.dynamic_slice_in_dim(source_rows, first_row, block_rows, 0)
        rows_in = jnp.where(my_layer == 0, start_rows, recv_rows)
        row_attn = lax.dynamic_slice_in_dim(scale_attn, first_row, block_rows, 0)
        normed = (rows_in * row_attn[:, None]).astype(jnp.bfloat16)
        values = halves(
            jnp.dot(columns(normed), value_weight, preferred_element_type=jnp.float32)
        ).astype(jnp.bfloat16)
        value_cache = values
        query_pos = first_pos + jnp.arange(block_rows, dtype=jnp.int32)
        prompt_len = lax.dynamic_index_in_dim(lengths, prompt_num, 0, keepdims=False)
        keep_keys = (positions[None, :] <= query_pos[:, None]) & (positions[None, :] < prompt_len)
        block_pat = lax.dynamic_slice(
            group_pat, (0, prompt_num, first_pos, 0), (per_group, 1, block_rows, seq_len)
        )[:, 0]
        block_pat = jnp.where(keep_keys[None], block_pat, jnp.zeros_like(block_pat))
        head_out = (
            jnp.einsum("uqk,kc->qcu", block_pat, value_cache, preferred_element_type=jnp.float32)
            .astype(jnp.bfloat16)
            .reshape(block_rows, -1)
        )
        attention = add_heads(lax.all_gather(head_out, "feat", axis=1, tiled=True))
        middle = rows_in + attention
        row_mlp = lax.dynamic_slice_in_dim(scale_mlp, first_row, block_rows, 0)
        normed_mlp = (middle * row_mlp[:, None]).astype(jnp.bfloat16)
        preact = (
            halves(jnp.dot(columns(normed_mlp), enc_rows, preferred_element_type=jnp.float32))
            + enc_shift
        )
        active = jnp.maximum(preact, 0.0)
        clamped = jnp.where(modes == 1, levels, jnp.where(modes == 2, active * levels, active))
        live_rows = query_pos < prompt_len
        block_feats = jnp.where(live_rows[:, None], clamped, 0.0).astype(jnp.bfloat16)
        writes = add_writes(lax.all_gather(block_feats, "feat", axis=1, tiled=True))
        error_block = lax.dynamic_slice_in_dim(error_rows, first_row, block_rows, 0)
        acc_in = jnp.where(my_layer == 0, jnp.zeros_like(links), links)
        running = acc_in + writes
        recon = lax.dynamic_index_in_dim(running, my_layer, 0, keepdims=False)
        rows_next = middle + recon + error_block
        recv_rows, links = passed_along((rows_next, running), "layer", 1)
        old_rows = lax.dynamic_slice_in_dim(kept_rows, first_row, block_rows, 0)
        kept_rows = lax.dynamic_update_slice_in_dim(
            kept_rows, jnp.where(is_live, rows_next, old_rows), first_row, 0
        )
        old_feats = lax.dynamic_slice_in_dim(kept_feats, first_row, block_rows, 0)
        kept_feats = lax.dynamic_update_slice_in_dim(
            kept_feats, jnp.where(is_live, block_feats, old_feats), first_row, 0
        )
        return (recv_rows, links, value_cache, kept_rows, kept_feats)

    link_start = jnp.zeros((layer_count, block_rows, width_cols), jnp.float32)
    initial = (
        jnp.zeros((block_rows, width_cols), jnp.float32),
        link_start,
        jnp.zeros((seq_len, kv_cols), jnp.bfloat16),
        jnp.zeros((total_rows, width_cols), jnp.float32),
        jnp.zeros((total_rows, block_len), jnp.bfloat16),
    )
    final = lax.fori_loop(0, section_count, section, initial)
    return (final[3][None, :, None, :], final[4][None])


def solution(mesh):
    return jax.shard_map(
        local,
        mesh=mesh,
        in_specs=(
            P("groups", "tok", "feat"),
            P("layer", "groups"),
            P("layer", "groups"),
            P("layer", None, "groups", None, None),
            P("groups"),
            P("layer", "tok", None, "feat"),
            P("layer", None, None, None, "tok", "feat"),
            P("layer", "tok", None, "feat"),
            P("layer", "feat"),
            P("layer", None, None, "tok", "feat"),
            P("layer", "groups", "tok", "feat"),
            P("layer", "feat"),
            P("layer", "feat"),
            P(),
            P("layer", "feat"),
        ),
        out_specs=(P("layer", "groups", "tok", "feat"), P("layer", "groups", "feat")),
        check_vma=False,
    )
```

profile of v0, /device:TPU:0, one launch (start us, length us, event | category | flops | bytes accessed | tf_op | source)
XLA Modules:
  0.0 265.3 jit_solution(8046609144955655287)
XLA Ops:
  0.7 0.9 copy-done
  3.0 0.7 select_reduce_fusion
  3.7 6.1 %copy.43 = bf16[1,4,256,2,1,448]{5,3,2,1,4,0:T(2,128)(2,1)} copy(bf16[1,4,256,2,1,448]{2,5,4,3,1,0:T(8,128)(2,1)} %param.23) | data formatting | bytes 3670016 | tf_op args[6]
  9.9 3.5 %reshape_squeeze.9 = bf16[2048,448]{1,0:T(8,128)(2,1)S(1)} reshape(bf16[1,4,256,2,1,448]{5,3,2,1,4,0:T(2,128)(2,1)} %copy.43) | data formatting | bytes 3670016 | tf_op jit(solution)/shard_map/reshape;squeeze | solution.py:61
  13.5 0.8 copy.44
  14.4 0.7 broadcast.116
  15.1 0.7 broadcast_in_dim.131
  15.9 247.6 %while.23 = (s32[]{:T(128)}, f32[64,448]{1,0:T(8,128)S(1)}, f32[2,64,448]{2,1,0:T(8,128)}, f32[128,448]{1,0:T(8,128)}, bf16[128,128]{1,0:T(8,128)(2,1)S(1)}, /*i...) while((s32[]{:T(128)}, f32[64,448]{1,0:T(8,128)S(1)}, ...), condition=%wide.region_4.5_spmd.clone.clone, body=%wide.region_1.4_spmd.clone.clone.sunk | while | flops 268976448 | bytes 11732813 | solution.py:150
  16.1 15.7 %all-gather.6 = bf16[4,448,64]{1,2,0:T(8,128)(2,1)S(1)} all-gather(bf16[1,448,64]{1,2,0:T(8,128)(2,1)S(1)} %fusion.57), channel_id=1, replica_groups=mesh['groups'=2,'feat'=4,'layer'=2,'tok'=2] {'feat'}, dimensions={0}, use_global_device_ids=true | all-gather | bytes 286720 | tf_op jit(solution)/shard_map/while/body/eval_jaxpr/all_gather | solution.py:14
  32.2 1.5 fusion.58
  33.7 3.6 %psum.34 = bf16[64,256]{1,0:T(8,128)(2,1)S(1)} all-reduce(f32[64,256]{1,0:T(8,128)S(1)} %fusion.58), channel_id=1, replica_groups=mesh['groups'=2,'feat'=4,'layer'=2,'tok'=2] {'tok'}, use_global_device_ids=true, to_apply=%region_2.2 | all-reduce | flops 16384 | bytes 98304 | tf_op jit(solution)/shard_map/while/body/eval_jaxpr/psum | solution.py:18
  38.9 16.6 %all_gather.48 = bf16[64,2048]{0,1:T(8,128)(2,1)S(1)} all-gather(bf16[64,512]{0,1:T(8,128)(2,1)S(1)} %bitcast.101), channel_id=1, replica_groups=mesh['groups'=2,'feat'=4,'layer'=2,'tok'=2] {'feat'}, dimensions={1}, use_global_device_ids=true | all-gather | bytes 327680 | tf_op jit(solution)/shard_map/while/body/eval_jaxpr/all_gather | solution.py:113
  56.2 14.5 %all-gather.7 = bf16[4,448,64]{1,2,0:T(8,128)(2,1)S(1)} all-gather(bf16[1,448,64]{1,2,0:T(8,128)(2,1)S(1)} %fusion.61), channel_id=1, replica_groups=mesh['groups'=2,'feat'=4,'layer'=2,'tok'=2] {'feat'}, dimensions={0}, use_global_device_ids=true | all-gather | bytes 286720 | tf_op jit(solution)/shard_map/while/body/eval_jaxpr/all_gather | solution.py:14
  71.2 1.2 fusion.62
  72.4 3.4 %psum.35 = f32[64,128]{1,0:T(8,128)S(1)} all-reduce(f32[64,128]{1,0:T(8,128)S(1)} %fusion.62), channel_id=1, replica_groups=mesh['groups'=2,'feat'=4,'layer'=2,'tok'=2] {'tok'}, use_global_device_ids=true, to_apply=%region_3.3 | all-reduce | flops 8192 | bytes 65536 | tf_op jit(solution)/shard_map/while/body/eval_jaxpr/psum | solution.py:18
  76.0 12.0 %all_gather.49 = bf16[64,512]{1,0:T(8,128)(2,1)S(1)} all-gather(bf16[64,128]{1,0:T(8,128)(2,1)S(1)} %get-tuple-element.762), channel_id=1, replica_groups=mesh['groups'=2,'feat'=4,'layer'=2,'tok'=2] {'feat'}, dimensions={1}, use_global_device_ids=true | all-gather | bytes 81920 | tf_op jit(solution)/shard_map/while/body/eval_jaxpr/all_gather | solution.py:125
  88.0 1.6 fusion.63
  89.5 4.1 %collective-permute-start.1 = (f32[2,64,448]{2,1,0:T(8,128)S(1)}, f32[2,64,448]{2,1,0:T(8,128)}, u32[]{:S(2)}, u32[]{:S(2)}) collective-permute-start(f32[2,64,448]{2,1,0:T(8,128)S(1)} %fusion.63), channel_id=1, source_target_pairs={{0,2},{1,3},{4,6},{5,7},{8,10},{9,11},{12,14},{13,15},{16,18},{17,... | collective-permute-start | bytes 688136 | tf_op jit(solution)/shard_map/while/body/eval_jaxpr/ppermute | solution.py:10
  93.7 1.6 select_dynamic-update-slice_fusion.5
  95.3 1.3 collective-permute-start
  96.6 3.0 %collective-permute-done = f32[64,448]{1,0:T(8,128)S(1)} collective-permute-done((f32[64,448]{1,0:T(8,128)S(1)}, f32[64,448]{1,0:T(8,128)S(1)}, u32[]{:S(2)}, u32[]{:S(2)}) %collective-permute-start) | collective-permute-done | bytes 114720 | tf_op jit(solution)/shard_map/while/body/eval_jaxpr/ppermute | solution.py:10
  99.8 14.3 %all-gather.6 = bf16[4,448,64]{1,2,0:T(8,128)(2,1)S(1)} all-gather(bf16[1,448,64]{1,2,0:T(8,128)(2,1)S(1)} %fusion.57), channel_id=1, replica_groups=mesh['groups'=2,'feat'=4,'layer'=2,'tok'=2] {'feat'}, dimensions={0}, use_global_device_ids=true | all-gather | bytes 286720 | tf_op jit(solution)/shard_map/while/body/eval_jaxpr/all_gather | solution.py:14
  114.6 1.5 fusion.58
  116.1 3.6 %psum.34 = bf16[64,256]{1,0:T(8,128)(2,1)S(1)} all-reduce(f32[64,256]{1,0:T(8,128)S(1)} %fusion.58), channel_id=1, replica_groups=mesh['groups'=2,'feat'=4,'layer'=2,'tok'=2] {'tok'}, use_global_device_ids=true, to_apply=%region_2.2 | all-reduce | flops 16384 | bytes 98304 | tf_op jit(solution)/shard_map/while/body/eval_jaxpr/psum | solution.py:18
  121.3 16.2 %all_gather.48 = bf16[64,2048]{0,1:T(8,128)(2,1)S(1)} all-gather(bf16[64,512]{0,1:T(8,128)(2,1)S(1)} %bitcast.101), channel_id=1, replica_groups=mesh['groups'=2,'feat'=4,'layer'=2,'tok'=2] {'feat'}, dimensions={1}, use_global_device_ids=true | all-gather | bytes 327680 | tf_op jit(solution)/shard_map/while/body/eval_jaxpr/all_gather | solution.py:113
  138.2 13.8 %all-gather.7 = bf16[4,448,64]{1,2,0:T(8,128)(2,1)S(1)} all-gather(bf16[1,448,64]{1,2,0:T(8,128)(2,1)S(1)} %fusion.61), channel_id=1, replica_groups=mesh['groups'=2,'feat'=4,'layer'=2,'tok'=2] {'feat'}, dimensions={0}, use_global_device_ids=true | all-gather | bytes 286720 | tf_op jit(solution)/shard_map/while/body/eval_jaxpr/all_gather | solution.py:14
  152.5 1.2 fusion.62
  153.7 3.4 %psum.35 = f32[64,128]{1,0:T(8,128)S(1)} all-reduce(f32[64,128]{1,0:T(8,128)S(1)} %fusion.62), channel_id=1, replica_groups=mesh['groups'=2,'feat'=4,'layer'=2,'tok'=2] {'tok'}, use_global_device_ids=true, to_apply=%region_3.3 | all-reduce | flops 8192 | bytes 65536 | tf_op jit(solution)/shard_map/while/body/eval_jaxpr/psum | solution.py:18
  157.3 12.0 %all_gather.49 = bf16[64,512]{1,0:T(8,128)(2,1)S(1)} all-gather(bf16[64,128]{1,0:T(8,128)(2,1)S(1)} %get-tuple-element.762), channel_id=1, replica_groups=mesh['groups'=2,'feat'=4,'layer'=2,'tok'=2] {'feat'}, dimensions={1}, use_global_device_ids=true | all-gather | bytes 81920 | tf_op jit(solution)/shard_map/while/body/eval_jaxpr/all_gather | solution.py:125
  169.3 1.6 fusion.63
  170.8 5.0 %collective-permute-start.1 = (f32[2,64,448]{2,1,0:T(8,128)S(1)}, f32[2,64,448]{2,1,0:T(8,128)}, u32[]{:S(2)}, u32[]{:S(2)}) collective-permute-start(f32[2,64,448]{2,1,0:T(8,128)S(1)} %fusion.63), channel_id=1, source_target_pairs={{0,2},{1,3},{4,6},{5,7},{8,10},{9,11},{12,14},{13,15},{16,18},{17,... | collective-permute-start | bytes 688136 | tf_op jit(solution)/shard_map/while/body/eval_jaxpr/ppermute | solution.py:10
  175.9 1.7 select_dynamic-update-slice_fusion.5
  177.5 1.3 collective-permute-start
  178.8 3.0 %collective-permute-done = f32[64,448]{1,0:T(8,128)S(1)} collective-permute-done((f32[64,448]{1,0:T(8,128)S(1)}, f32[64,448]{1,0:T(8,128)S(1)}, u32[]{:S(2)}, u32[]{:S(2)}) %collective-permute-start) | collective-permute-done | bytes 114720 | tf_op jit(solution)/shard_map/while/body/eval_jaxpr/ppermute | solution.py:10
  182.0 13.8 %all-gather.6 = bf16[4,448,64]{1,2,0:T(8,128)(2,1)S(1)} all-gather(bf16[1,448,64]{1,2,0:T(8,128)(2,1)S(1)} %fusion.57), channel_id=1, replica_groups=mesh['groups'=2,'feat'=4,'layer'=2,'tok'=2] {'feat'}, dimensions={0}, use_global_device_ids=true | all-gather | bytes 286720 | tf_op jit(solution)/shard_map/while/body/eval_jaxpr/all_gather | solution.py:14
  196.3 1.5 fusion.58
  197.7 3.6 %psum.34 = bf16[64,256]{1,0:T(8,128)(2,1)S(1)} all-reduce(f32[64,256]{1,0:T(8,128)S(1)} %fusion.58), channel_id=1, replica_groups=mesh['groups'=2,'feat'=4,'layer'=2,'tok'=2] {'tok'}, use_global_device_ids=true, to_apply=%region_2.2 | all-reduce | flops 16384 | bytes 98304 | tf_op jit(solution)/shard_map/while/body/eval_jaxpr/psum | solution.py:18
  203.0 16.1 %all_gather.48 = bf16[64,2048]{0,1:T(8,128)(2,1)S(1)} all-gather(bf16[64,512]{0,1:T(8,128)(2,1)S(1)} %bitcast.101), channel_id=1, replica_groups=mesh['groups'=2,'feat'=4,'layer'=2,'tok'=2] {'feat'}, dimensions={1}, use_global_device_ids=true | all-gather | bytes 327680 | tf_op jit(solution)/shard_map/while/body/eval_jaxpr/all_gather | solution.py:113
  219.7 13.8 %all-gather.7 = bf16[4,448,64]{1,2,0:T(8,128)(2,1)S(1)} all-gather(bf16[1,448,64]{1,2,0:T(8,128)(2,1)S(1)} %fusion.61), channel_id=1, replica_groups=mesh['groups'=2,'feat'=4,'layer'=2,'tok'=2] {'feat'}, dimensions={0}, use_global_device_ids=true | all-gather | bytes 286720 | tf_op jit(solution)/shard_map/while/body/eval_jaxpr/all_gather | solution.py:14
  234.0 1.2 fusion.62
  235.3 3.4 %psum.35 = f32[64,128]{1,0:T(8,128)S(1)} all-reduce(f32[64,128]{1,0:T(8,128)S(1)} %fusion.62), channel_id=1, replica_groups=mesh['groups'=2,'feat'=4,'layer'=2,'tok'=2] {'tok'}, use_global_device_ids=true, to_apply=%region_3.3 | all-reduce | flops 8192 | bytes 65536 | tf_op jit(solution)/shard_map/while/body/eval_jaxpr/psum | solution.py:18
  238.8 12.0 %all_gather.49 = bf16[64,512]{1,0:T(8,128)(2,1)S(1)} all-gather(bf16[64,128]{1,0:T(8,128)(2,1)S(1)} %get-tuple-element.762), channel_id=1, replica_groups=mesh['groups'=2,'feat'=4,'layer'=2,'tok'=2] {'feat'}, dimensions={1}, use_global_device_ids=true | all-gather | bytes 81920 | tf_op jit(solution)/shard_map/while/body/eval_jaxpr/all_gather | solution.py:125
  250.8 1.6 fusion.63
  252.4 5.1 %collective-permute-start.1 = (f32[2,64,448]{2,1,0:T(8,128)S(1)}, f32[2,64,448]{2,1,0:T(8,128)}, u32[]{:S(2)}, u32[]{:S(2)}) collective-permute-start(f32[2,64,448]{2,1,0:T(8,128)S(1)} %fusion.63), channel_id=1, source_target_pairs={{0,2},{1,3},{4,6},{5,7},{8,10},{9,11},{12,14},{13,15},{16,18},{17,... | collective-permute-start | bytes 688136 | tf_op jit(solution)/shard_map/while/body/eval_jaxpr/ppermute | solution.py:10
  257.5 1.7 select_dynamic-update-slice_fusion.5
  259.1 1.3 collective-permute-start
  260.4 3.0 %collective-permute-done = f32[64,448]{1,0:T(8,128)S(1)} collective-permute-done((f32[64,448]{1,0:T(8,128)S(1)}, f32[64,448]{1,0:T(8,128)S(1)}, u32[]{:S(2)}, u32[]{:S(2)}) %collective-permute-start) | collective-permute-done | bytes 114720 | tf_op jit(solution)/shard_map/while/body/eval_jaxpr/ppermute | solution.py:10
  263.5 1.8 copy.45
  (71 shorter events, 11.2 us)
Async XLA Ops:
  0.6 1.0 copy-start
  9.8 3.5 %copy-start.2 = (f32[128,1,448]{0,2,1:T(8,128)S(1)}, f32[128,1,448]{0,2,1:T(8,128)}, u32[]{:S(2)}) copy-start(f32[128,1,448]{0,2,1:T(8,128)} %param.17) | copy-start | bytes 688132
  9.8 3.7 %copy-start.3 = (f32[1,128,1,448]{1,3,2,0:T(8,128)S(1)}, f32[1,128,1,448]{1,3,2,0:T(8,128)}, u32[]{:S(2)}) copy-start(f32[1,128,1,448]{1,3,2,0:T(8,128)} %param.27) | copy-start | bytes 688132
  9.8 6.0 %copy-start.4 = (f32[1,128]{1,0:T(1,128)S(1)}, f32[1,128]{1,0:T(1,128)}, u32[]{:S(2)}) copy-start(f32[1,128]{1,0:T(1,128)} %param.25) | copy-start | bytes 1540
  9.8 6.0 %copy-start.5 = (f32[1,128]{1,0:T(1,128)S(1)}, f32[1,128]{1,0:T(1,128)}, u32[]{:S(2)}) copy-start(f32[1,128]{1,0:T(1,128)} %param.18) | copy-start | bytes 1540
  9.9 6.0 %copy-start.6 = (s32[2]{0:T(128)S(1)}, s32[2]{0:T(128)}, u32[]{:S(2)}) copy-start(s32[2]{0:T(128)} %param.21) | copy-start | bytes 28
  9.9 6.0 %copy-start.7 = (f32[1,128]{1,0:T(1,128)S(1)}, f32[1,128]{1,0:T(1,128)}, u32[]{:S(2)}) copy-start(f32[1,128]{1,0:T(1,128)} %param.19) | copy-start | bytes 1540
  89.5 10.1 %collective-permute-start.1 = (f32[2,64,448]{2,1,0:T(8,128)S(1)}, f32[2,64,448]{2,1,0:T(8,128)}, u32[]{:S(2)}, u32[]{:S(2)}) collective-permute-start(f32[2,64,448]{2,1,0:T(8,128)S(1)} %fusion.63), channel_id=1, source_target_pairs={{0,2},{1,3},{4,6},{5,7},{8,10},{9,11},{12,14},{13,15},{16,18},{17,... | collective-permute-start | bytes 688136 | tf_op jit(solution)/shard_map/while/body/eval_jaxpr/ppermute | solution.py:10
  95.3 4.3 %collective-permute-start = (f32[64,448]{1,0:T(8,128)S(1)}, f32[64,448]{1,0:T(8,128)S(1)}, u32[]{:S(2)}, u32[]{:S(2)}) collective-permute-start(f32[64,448]{1,0:T(8,128)S(1)} %get-tuple-element.763), channel_id=1, source_target_pairs={{0,2},{1,3},{4,6},{5,7},{8,10},{9,11},{12,14},{13,15},{16,18},{17,... | collective-permute-start | bytes 344072 | tf_op jit(solution)/shard_map/while/body/eval_jaxpr/ppermute | solution.py:10
  170.8 11.0 %collective-permute-start.1 = (f32[2,64,448]{2,1,0:T(8,128)S(1)}, f32[2,64,448]{2,1,0:T(8,128)}, u32[]{:S(2)}, u32[]{:S(2)}) collective-permute-start(f32[2,64,448]{2,1,0:T(8,128)S(1)} %fusion.63), channel_id=1, source_target_pairs={{0,2},{1,3},{4,6},{5,7},{8,10},{9,11},{12,14},{13,15},{16,18},{17,... | collective-permute-start | bytes 688136 | tf_op jit(solution)/shard_map/while/body/eval_jaxpr/ppermute | solution.py:10
  177.5 4.3 %collective-permute-start = (f32[64,448]{1,0:T(8,128)S(1)}, f32[64,448]{1,0:T(8,128)S(1)}, u32[]{:S(2)}, u32[]{:S(2)}) collective-permute-start(f32[64,448]{1,0:T(8,128)S(1)} %get-tuple-element.763), channel_id=1, source_target_pairs={{0,2},{1,3},{4,6},{5,7},{8,10},{9,11},{12,14},{13,15},{16,18},{17,... | collective-permute-start | bytes 344072 | tf_op jit(solution)/shard_map/while/body/eval_jaxpr/ppermute | solution.py:10
  252.4 11.1 %collective-permute-start.1 = (f32[2,64,448]{2,1,0:T(8,128)S(1)}, f32[2,64,448]{2,1,0:T(8,128)}, u32[]{:S(2)}, u32[]{:S(2)}) collective-permute-start(f32[2,64,448]{2,1,0:T(8,128)S(1)} %fusion.63), channel_id=1, source_target_pairs={{0,2},{1,3},{4,6},{5,7},{8,10},{9,11},{12,14},{13,15},{16,18},{17,... | collective-permute-start | bytes 688136 | tf_op jit(solution)/shard_map/while/body/eval_jaxpr/ppermute | solution.py:10
  259.1 4.3 %collective-permute-start = (f32[64,448]{1,0:T(8,128)S(1)}, f32[64,448]{1,0:T(8,128)S(1)}, u32[]{:S(2)}, u32[]{:S(2)}) collective-permute-start(f32[64,448]{1,0:T(8,128)S(1)} %get-tuple-element.763), channel_id=1, source_target_pairs={{0,2},{1,3},{4,6},{5,7},{8,10},{9,11},{12,14},{13,15},{16,18},{17,... | collective-permute-start | bytes 344072 | tf_op jit(solution)/shard_map/while/body/eval_jaxpr/ppermute | solution.py:10
  263.5 1.8 copy-start.1
where the time goes:
time: 266 us; the launch traced here: 265 us
  blocking collectives  192 us (72%)
  local copies, waits for them, and re-layouts  21.1 us (8%)
  starting transfers between devices  18.2 us (7%)
  matrix products  14.7 us (6%)
  waiting for transfers between devices  9.11 us (3%)
  other arithmetic  8.55 us (3%)
    all_gather x6, blocking collectives, columns(): return lax.all_gather(normed_rows, 'feat', axis=1, tiled=True)  85.9 us
    all_gather x3, blocking collectives, section(): attention = add_heads(lax.all_gather(head_out, 'feat', axis=1, tiled=True))  48.9 us
    all_gather x3, blocking collectives, section(): writes = add_writes(lax.all_gather(block_feats, 'feat', axis=1, tiled=True))  36 us
    psum x6, blocking collectives, halves(): return lax.psum(partial_sum, 'tok')  21.1 us
    ppermute x6, starting transfers between devices, passed_along(): lax.ppermute(value, axis, [(source, source + steps) for source in range(i...  18.2 us
    ppermute x6, waiting for transfers between devices, passed_along(): lax.ppermute(value, axis, [(source, source + steps) for source in range(i...  9.11 us
    unnamed x19, local copies, waits for them, and re-layouts  8.06 us
  transfers between devices with their start and end apart: 6, of which 3 were waited for; matrix products, arithmetic and copies ran while one was open for 2% of the time, Pallas kernels for 0%

commit v1 on v0

--- a/solution.py
+++ b/solution.py
@@ -2,6 +2,11 @@
 import jax.numpy as jnp
 from jax import lax
 from jax.sharding import PartitionSpec as P
+
+
+def order_clusters(xin):
+    out_arr = lax.all_gather(xin, "tok").sum(axis=0)
+    return out_arr
 
 
 def passed_along(value, axis, steps):
@@ -15,7 +20,7 @@
 
 
 def halves(partial_sum):
-    return lax.psum(partial_sum, "tok")
+    return order_clusters(partial_sum)
 
 
 def pick_block(lookup_table, chosen, block_len):

time: 266 us -> 256 us (0.962)
  blocking collectives: 192 us -> 181 us
    psum x6 -> x0, blocking collectives: 21.1 us -> none  [halves(): return lax.psum(partial_sum, 'tok')]
    all_gather x0 -> x6, blocking collectives: none -> 11.3 us  [order_clusters(): out_arr = lax.all_gather(xin, 'tok').sum(axis=0)]
where the time goes in v1:
time: 256 us; the launch traced here: 255 us
  blocking collectives  181 us (71%)
  local copies, waits for them, and re-layouts  21 us (8%)
  starting transfers between devices  18.3 us (7%)
  matrix products  14.7 us (6%)
  waiting for transfers between devices  9.11 us (4%)
  other arithmetic  8.6 us (3%)
    all_gather x6, blocking collectives, columns(): return lax.all_gather(normed_rows, 'feat', axis=1, tiled=True)  85.9 us
    all_gather x3, blocking collectives, section(): attention = add_heads(lax.all_gather(head_out, 'feat', axis=1, tiled=True))  48.3 us
    all_gather x3, blocking collectives, section(): writes = add_writes(lax.all_gather(block_feats, 'feat', axis=1, tiled=True))  36 us
    ppermute x6, starting transfers between devices, passed_along(): lax.ppermute(value, axis, [(source, source + steps) for source in range(i...  18.3 us
    all_gather x6, blocking collectives, order_clusters(): out_arr = lax.all_gather(xin, 'tok').sum(axis=0)  11.3 us
    ppermute x6, waiting for transfers between devices, passed_along(): lax.ppermute(value, axis, [(source, source + steps) for source in range(i...  9.11 us
    unnamed x19, local copies, waits for them, and re-layouts  8.06 us
  transfers between devices with their start and end apart: 6, of which 3 were waited for; matrix products, arithmetic and copies ran while one was open for 2% of the time, Pallas kernels for 0%

profile of v1, /device:TPU:0, one launch (start us, length us, event | category | flops | bytes accessed | tf_op | source)
XLA Modules:
  0.0 255.0 jit_solution(11428508432403045698)
XLA Ops:
  0.7 0.9 copy-done
  3.0 0.7 select_reduce_fusion
  3.7 6.1 %copy.43 = bf16[1,4,256,2,1,448]{5,3,2,1,4,0:T(2,128)(2,1)} copy(bf16[1,4,256,2,1,448]{2,5,4,3,1,0:T(8,128)(2,1)} %param.23) | data formatting | bytes 3670016 | tf_op args[6]
  9.9 3.5 %reshape_squeeze.9 = bf16[2048,448]{1,0:T(8,128)(2,1)S(1)} reshape(bf16[1,4,256,2,1,448]{5,3,2,1,4,0:T(2,128)(2,1)} %copy.43) | data formatting | bytes 3670016 | tf_op jit(solution)/shard_map/reshape;squeeze | solution.py:66
  13.5 0.8 copy.44
  14.4 0.7 broadcast.116
  15.1 0.7 broadcast_in_dim.131
  15.9 237.3 %while.23 = (s32[]{:T(128)}, f32[64,448]{1,0:T(8,128)S(1)}, f32[2,64,448]{2,1,0:T(8,128)}, f32[128,448]{1,0:T(8,128)}, bf16[128,128]{1,0:T(8,128)(2,1)S(1)}, /*i...) while((s32[]{:T(128)}, f32[64,448]{1,0:T(8,128)S(1)}, ...), condition=%wide.region_4.5_spmd.clone.clone, body=%wide.region_1.4_spmd.clone.clone.sunk | while | flops 268976448 | bytes 12126045 | solution.py:155
  16.1 15.7 %all-gather.12 = bf16[4,448,64]{1,2,0:T(8,128)(2,1)S(1)} all-gather(bf16[1,448,64]{1,2,0:T(8,128)(2,1)S(1)} %fusion.57), channel_id=1, replica_groups=mesh['groups'=2,'feat'=4,'layer'=2,'tok'=2] {'feat'}, dimensions={0}, use_global_device_ids=true | all-gather | bytes 286720 | tf_op jit(solution)/shard_map/while/body/eval_jaxpr/all_gather | solution.py:19
  32.2 1.5 fusion.58
  33.7 1.9 all-gather.13
  37.2 16.4 %all_gather.92 = bf16[64,2048]{0,1:T(8,128)(2,1)S(1)} all-gather(bf16[64,512]{0,1:T(8,128)(2,1)S(1)} %bitcast.107), channel_id=1, replica_groups=mesh['groups'=2,'feat'=4,'layer'=2,'tok'=2] {'feat'}, dimensions={1}, use_global_device_ids=true | all-gather | bytes 327680 | tf_op jit(solution)/shard_map/while/body/eval_jaxpr/all_gather | solution.py:118
  54.3 14.5 %all-gather.14 = bf16[4,448,64]{1,2,0:T(8,128)(2,1)S(1)} all-gather(bf16[1,448,64]{1,2,0:T(8,128)(2,1)S(1)} %fusion.61), channel_id=1, replica_groups=mesh['groups'=2,'feat'=4,'layer'=2,'tok'=2] {'feat'}, dimensions={0}, use_global_device_ids=true | all-gather | bytes 286720 | tf_op jit(solution)/shard_map/while/body/eval_jaxpr/all_gather | solution.py:19
  69.3 1.2 fusion.62
  70.5 1.9 all-gather.15
  72.5 12.0 %all_gather.93 = bf16[64,512]{1,0:T(8,128)(2,1)S(1)} all-gather(bf16[64,128]{1,0:T(8,128)(2,1)S(1)} %get-tuple-element.762), channel_id=1, replica_groups=mesh['groups'=2,'feat'=4,'layer'=2,'tok'=2] {'feat'}, dimensions={1}, use_global_device_ids=true | all-gather | bytes 81920 | tf_op jit(solution)/shard_map/while/body/eval_jaxpr/all_gather | solution.py:130
  84.5 1.6 fusion.63
  86.1 4.1 %collective-permute-start.1 = (f32[2,64,448]{2,1,0:T(8,128)S(1)}, f32[2,64,448]{2,1,0:T(8,128)}, u32[]{:S(2)}, u32[]{:S(2)}) collective-permute-start(f32[2,64,448]{2,1,0:T(8,128)S(1)} %fusion.63), channel_id=1, source_target_pairs={{0,2},{1,3},{4,6},{5,7},{8,10},{9,11},{12,14},{13,15},{16,18},{17,... | collective-permute-start | bytes 688136 | tf_op jit(solution)/shard_map/while/body/eval_jaxpr/ppermute | solution.py:15
  90.2 1.6 select_dynamic-update-slice_fusion.5
  91.8 1.3 collective-permute-start
  93.1 3.0 %collective-permute-done = f32[64,448]{1,0:T(8,128)S(1)} collective-permute-done((f32[64,448]{1,0:T(8,128)S(1)}, f32[64,448]{1,0:T(8,128)S(1)}, u32[]{:S(2)}, u32[]{:S(2)}) %collective-permute-start) | collective-permute-done | bytes 114720 | tf_op jit(solution)/shard_map/while/body/eval_jaxpr/ppermute | solution.py:15
  96.3 14.3 %all-gather.12 = bf16[4,448,64]{1,2,0:T(8,128)(2,1)S(1)} all-gather(bf16[1,448,64]{1,2,0:T(8,128)(2,1)S(1)} %fusion.57), channel_id=1, replica_groups=mesh['groups'=2,'feat'=4,'layer'=2,'tok'=2] {'feat'}, dimensions={0}, use_global_device_ids=true | all-gather | bytes 286720 | tf_op jit(solution)/shard_map/while/body/eval_jaxpr/all_gather | solution.py:19
  111.1 1.5 fusion.58
  112.6 1.9 all-gather.13
  116.1 15.9 %all_gather.92 = bf16[64,2048]{0,1:T(8,128)(2,1)S(1)} all-gather(bf16[64,512]{0,1:T(8,128)(2,1)S(1)} %bitcast.107), channel_id=1, replica_groups=mesh['groups'=2,'feat'=4,'layer'=2,'tok'=2] {'feat'}, dimensions={1}, use_global_device_ids=true | all-gather | bytes 327680 | tf_op jit(solution)/shard_map/while/body/eval_jaxpr/all_gather | solution.py:118
  132.7 13.8 %all-gather.14 = bf16[4,448,64]{1,2,0:T(8,128)(2,1)S(1)} all-gather(bf16[1,448,64]{1,2,0:T(8,128)(2,1)S(1)} %fusion.61), channel_id=1, replica_groups=mesh['groups'=2,'feat'=4,'layer'=2,'tok'=2] {'feat'}, dimensions={0}, use_global_device_ids=true | all-gather | bytes 286720 | tf_op jit(solution)/shard_map/while/body/eval_jaxpr/all_gather | solution.py:19
  147.0 1.2 fusion.62
  148.3 1.9 all-gather.15
  150.2 12.0 %all_gather.93 = bf16[64,512]{1,0:T(8,128)(2,1)S(1)} all-gather(bf16[64,128]{1,0:T(8,128)(2,1)S(1)} %get-tuple-element.762), channel_id=1, replica_groups=mesh['groups'=2,'feat'=4,'layer'=2,'tok'=2] {'feat'}, dimensions={1}, use_global_device_ids=true | all-gather | bytes 81920 | tf_op jit(solution)/shard_map/while/body/eval_jaxpr/all_gather | solution.py:130
  162.2 1.6 fusion.63
  163.8 5.2 %collective-permute-start.1 = (f32[2,64,448]{2,1,0:T(8,128)S(1)}, f32[2,64,448]{2,1,0:T(8,128)}, u32[]{:S(2)}, u32[]{:S(2)}) collective-permute-start(f32[2,64,448]{2,1,0:T(8,128)S(1)} %fusion.63), channel_id=1, source_target_pairs={{0,2},{1,3},{4,6},{5,7},{8,10},{9,11},{12,14},{13,15},{16,18},{17,... | collective-permute-start | bytes 688136 | tf_op jit(solution)/shard_map/while/body/eval_jaxpr/ppermute | solution.py:15
  169.0 1.7 select_dynamic-update-slice_fusion.5
  170.6 1.3 collective-permute-start
  171.9 3.0 %collective-permute-done = f32[64,448]{1,0:T(8,128)S(1)} collective-permute-done((f32[64,448]{1,0:T(8,128)S(1)}, f32[64,448]{1,0:T(8,128)S(1)}, u32[]{:S(2)}, u32[]{:S(2)}) %collective-permute-start) | collective-permute-done | bytes 114720 | tf_op jit(solution)/shard_map/while/body/eval_jaxpr/ppermute | solution.py:15
  175.1 13.8 %all-gather.12 = bf16[4,448,64]{1,2,0:T(8,128)(2,1)S(1)} all-gather(bf16[1,448,64]{1,2,0:T(8,128)(2,1)S(1)} %fusion.57), channel_id=1, replica_groups=mesh['groups'=2,'feat'=4,'layer'=2,'tok'=2] {'feat'}, dimensions={0}, use_global_device_ids=true | all-gather | bytes 286720 | tf_op jit(solution)/shard_map/while/body/eval_jaxpr/all_gather | solution.py:19
  189.4 1.4 fusion.58
  190.8 1.9 all-gather.13
  194.4 16.0 %all_gather.92 = bf16[64,2048]{0,1:T(8,128)(2,1)S(1)} all-gather(bf16[64,512]{0,1:T(8,128)(2,1)S(1)} %bitcast.107), channel_id=1, replica_groups=mesh['groups'=2,'feat'=4,'layer'=2,'tok'=2] {'feat'}, dimensions={1}, use_global_device_ids=true | all-gather | bytes 327680 | tf_op jit(solution)/shard_map/while/body/eval_jaxpr/all_gather | solution.py:118
  211.0 13.8 %all-gather.14 = bf16[4,448,64]{1,2,0:T(8,128)(2,1)S(1)} all-gather(bf16[1,448,64]{1,2,0:T(8,128)(2,1)S(1)} %fusion.61), channel_id=1, replica_groups=mesh['groups'=2,'feat'=4,'layer'=2,'tok'=2] {'feat'}, dimensions={0}, use_global_device_ids=true | all-gather | bytes 286720 | tf_op jit(solution)/shard_map/while/body/eval_jaxpr/all_gather | solution.py:19
  225.3 1.2 fusion.62
  226.5 1.9 all-gather.15
  228.5 12.0 %all_gather.93 = bf16[64,512]{1,0:T(8,128)(2,1)S(1)} all-gather(bf16[64,128]{1,0:T(8,128)(2,1)S(1)} %get-tuple-element.762), channel_id=1, replica_groups=mesh['groups'=2,'feat'=4,'layer'=2,'tok'=2] {'feat'}, dimensions={1}, use_global_device_ids=true | all-gather | bytes 81920 | tf_op jit(solution)/shard_map/while/body/eval_jaxpr/all_gather | solution.py:130
  240.5 1.6 fusion.63
  242.1 5.2 %collective-permute-start.1 = (f32[2,64,448]{2,1,0:T(8,128)S(1)}, f32[2,64,448]{2,1,0:T(8,128)}, u32[]{:S(2)}, u32[]{:S(2)}) collective-permute-start(f32[2,64,448]{2,1,0:T(8,128)S(1)} %fusion.63), channel_id=1, source_target_pairs={{0,2},{1,3},{4,6},{5,7},{8,10},{9,11},{12,14},{13,15},{16,18},{17,... | collective-permute-start | bytes 688136 | tf_op jit(solution)/shard_map/while/body/eval_jaxpr/ppermute | solution.py:15
  247.2 1.7 select_dynamic-update-slice_fusion.5
  248.9 1.3 collective-permute-start
  250.2 3.0 %collective-permute-done = f32[64,448]{1,0:T(8,128)S(1)} collective-permute-done((f32[64,448]{1,0:T(8,128)S(1)}, f32[64,448]{1,0:T(8,128)S(1)}, u32[]{:S(2)}, u32[]{:S(2)}) %collective-permute-start) | collective-permute-done | bytes 114720 | tf_op jit(solution)/shard_map/while/body/eval_jaxpr/ppermute | solution.py:15
  253.2 1.8 copy.45
  (77 shorter events, 11.3 us)
Async XLA Ops:
  0.6 1.0 copy-start
  9.8 3.5 %copy-start.2 = (f32[128,1,448]{0,2,1:T(8,128)S(1)}, f32[128,1,448]{0,2,1:T(8,128)}, u32[]{:S(2)}) copy-start(f32[128,1,448]{0,2,1:T(8,128)} %param.17) | copy-start | bytes 688132
  9.8 3.7 %copy-start.3 = (f32[1,128,1,448]{1,3,2,0:T(8,128)S(1)}, f32[1,128,1,448]{1,3,2,0:T(8,128)}, u32[]{:S(2)}) copy-start(f32[1,128,1,448]{1,3,2,0:T(8,128)} %param.27) | copy-start | bytes 688132
  9.8 6.0 %copy-start.4 = (f32[1,128]{1,0:T(1,128)S(1)}, f32[1,128]{1,0:T(1,128)}, u32[]{:S(2)}) copy-start(f32[1,128]{1,0:T(1,128)} %param.25) | copy-start | bytes 1540
  9.8 6.0 %copy-start.5 = (f32[1,128]{1,0:T(1,128)S(1)}, f32[1,128]{1,0:T(1,128)}, u32[]{:S(2)}) copy-start(f32[1,128]{1,0:T(1,128)} %param.18) | copy-start | bytes 1540
  9.9 6.0 %copy-start.6 = (s32[2]{0:T(128)S(1)}, s32[2]{0:T(128)}, u32[]{:S(2)}) copy-start(s32[2]{0:T(128)} %param.21) | copy-start | bytes 28
  9.9 6.0 %copy-start.7 = (f32[1,128]{1,0:T(1,128)S(1)}, f32[1,128]{1,0:T(1,128)}, u32[]{:S(2)}) copy-start(f32[1,128]{1,0:T(1,128)} %param.19) | copy-start | bytes 1540
  86.1 10.1 %collective-permute-start.1 = (f32[2,64,448]{2,1,0:T(8,128)S(1)}, f32[2,64,448]{2,1,0:T(8,128)}, u32[]{:S(2)}, u32[]{:S(2)}) collective-permute-start(f32[2,64,448]{2,1,0:T(8,128)S(1)} %fusion.63), channel_id=1, source_target_pairs={{0,2},{1,3},{4,6},{5,7},{8,10},{9,11},{12,14},{13,15},{16,18},{17,... | collective-permute-start | bytes 688136 | tf_op jit(solution)/shard_map/while/body/eval_jaxpr/ppermute | solution.py:15
  91.8 4.3 %collective-permute-start = (f32[64,448]{1,0:T(8,128)S(1)}, f32[64,448]{1,0:T(8,128)S(1)}, u32[]{:S(2)}, u32[]{:S(2)}) collective-permute-start(f32[64,448]{1,0:T(8,128)S(1)} %get-tuple-element.763), channel_id=1, source_target_pairs={{0,2},{1,3},{4,6},{5,7},{8,10},{9,11},{12,14},{13,15},{16,18},{17,... | collective-permute-start | bytes 344072 | tf_op jit(solution)/shard_map/while/body/eval_jaxpr/ppermute | solution.py:15
  163.8 11.2 %collective-permute-start.1 = (f32[2,64,448]{2,1,0:T(8,128)S(1)}, f32[2,64,448]{2,1,0:T(8,128)}, u32[]{:S(2)}, u32[]{:S(2)}) collective-permute-start(f32[2,64,448]{2,1,0:T(8,128)S(1)} %fusion.63), channel_id=1, source_target_pairs={{0,2},{1,3},{4,6},{5,7},{8,10},{9,11},{12,14},{13,15},{16,18},{17,... | collective-permute-start | bytes 688136 | tf_op jit(solution)/shard_map/while/body/eval_jaxpr/ppermute | solution.py:15
  170.6 4.3 %collective-permute-start = (f32[64,448]{1,0:T(8,128)S(1)}, f32[64,448]{1,0:T(8,128)S(1)}, u32[]{:S(2)}, u32[]{:S(2)}) collective-permute-start(f32[64,448]{1,0:T(8,128)S(1)} %get-tuple-element.763), channel_id=1, source_target_pairs={{0,2},{1,3},{4,6},{5,7},{8,10},{9,11},{12,14},{13,15},{16,18},{17,... | collective-permute-start | bytes 344072 | tf_op jit(solution)/shard_map/while/body/eval_jaxpr/ppermute | solution.py:15
  242.1 11.1 %collective-permute-start.1 = (f32[2,64,448]{2,1,0:T(8,128)S(1)}, f32[2,64,448]{2,1,0:T(8,128)}, u32[]{:S(2)}, u32[]{:S(2)}) collective-permute-start(f32[2,64,448]{2,1,0:T(8,128)S(1)} %fusion.63), channel_id=1, source_target_pairs={{0,2},{1,3},{4,6},{5,7},{8,10},{9,11},{12,14},{13,15},{16,18},{17,... | collective-permute-start | bytes 688136 | tf_op jit(solution)/shard_map/while/body/eval_jaxpr/ppermute | solution.py:15
  248.9 4.3 %collective-permute-start = (f32[64,448]{1,0:T(8,128)S(1)}, f32[64,448]{1,0:T(8,128)S(1)}, u32[]{:S(2)}, u32[]{:S(2)}) collective-permute-start(f32[64,448]{1,0:T(8,128)S(1)} %get-tuple-element.763), channel_id=1, source_target_pairs={{0,2},{1,3},{4,6},{5,7},{8,10},{9,11},{12,14},{13,15},{16,18},{17,... | collective-permute-start | bytes 344072 | tf_op jit(solution)/shard_map/while/body/eval_jaxpr/ppermute | solution.py:15
  253.2 1.8 copy-start.1
